TPU v7x, 32 devices: a whole 2x2x4 slice. The times are simulated.
32 devices in a mesh: dp: 8 (over y, x, core), tensor: 4 (over z).
Axes of the slice: x: 2, y: 2, z: 4, core: 2. Of those that a mesh axis runs over, the one named last changes fastest.
Arguments:
- layer_input: bfloat16 [2048, 8, 768], P('tensor', 'dp'), may hold values from -6 to 6
- segments: int32 [8, 2048], P('dp'), may hold values from 0 to 64, as said below
- qkv_weight: bfloat16 [768, 2304], P(None, 'tensor'), may hold values from -0.21875 to 0.21875
- out_weight: bfloat16 [768, 768], P('tensor'), may hold values from -1.25 to 1.25
- gate_weight: bfloat16 [768, 3072], P(None, 'tensor'), may hold values from -0.21875 to 0.21875
- up_weight: bfloat16 [768, 3072], P(None, 'tensor'), may hold values from -0.21875 to 0.21875
- down_weight: bfloat16 [3072, 768], P('tensor'), may hold values from -0.109375 to 0.109375
- norm_params: float32 [4, 768], replicated, may hold values from -1.2 to 1.5, as said below
- cotangent: bfloat16 [2048, 8, 768], P('tensor', 'dp'), may hold values from -6 to 6
Outputs:
- layer_output: bfloat16 [2048, 8, 768], P('tensor', 'dp')
- input_grad: float32 [2048, 8, 768], P('tensor', 'dp')
- qkv_grad: float32 [768, 2304], P(None, 'tensor')
- out_grad: float32 [768, 768], P('tensor')
- gate_grad: float32 [768, 3072], P(None, 'tensor')
- up_grad: float32 [768, 3072], P(None, 'tensor')
- down_grad: float32 [3072, 768], P('tensor')
- norm_grads: float32 [4, 768], replicated
Inputs may be any that keep to these rules, and one draw needn't show every extreme that they name: `segments`: in each row, segment numbers never fall and each document's positions are contiguous; every document of a row has 20 or more positions; positions after the row's last document hold 64 (padding). Some row is one document of 2048 tokens, some row ends in padding. `norm_params`: rows 0 and 2 are gains, rows 1 and 3 are biases.
All inputs are finite; a program needn't handle non-finite values.
Results may differ from a plain program's by a relative error of at most 0.023.
Values may be sent and summed in bfloat16 or wider, within the bound.
No kernel may reach another device: no remote copies, remote signals or barrier semaphores. Data moves between devices by JAX's collectives and lax.ppermute only.
A program may use at most 128 MiB of HBM per device.

v0:
```python
import jax
import jax.numpy as jnp
from jax import lax
from jax.sharding import PartitionSpec as P

HEAD_DIM = 64
MAXDOCS = 64
EPSILON = 1e-05
ROPE_BASE = 1000.0
NEGATIVE = -1e30


def layer_norm(total, gain, bias):
    center = jnp.mean(total, axis=-1, keepdims=True)
    shifted = total - center
    spread = jnp.mean(shifted * shifted, axis=-1, keepdims=True)
    return shifted * lax.rsqrt(spread + EPSILON) * gain + bias


def positions_of(segment_row):
    labels = jnp.arange(MAXDOCS + 1, dtype=jnp.int32)
    chosen = segment_row[:, None] == labels[None, :]
    counts = jnp.sum(chosen.astype(jnp.int32), axis=0, dtype=jnp.int32)
    starts = jnp.cumsum(counts, dtype=jnp.int32) - counts
    first = jnp.sum(jnp.where(chosen, starts[None, :], 0), axis=1, dtype=jnp.int32)
    return jnp.arange(segment_row.shape[0], dtype=jnp.int32) - first


def rotary_tables(positions, depth):
    half = depth // 2
    powers = jnp.arange(half, dtype=jnp.float32) * (-2.0 / depth)
    inverse = ROPE_BASE**powers
    angles = positions.astype(jnp.float32)[..., None] * inverse
    return (jnp.cos(angles), jnp.sin(angles))


def rotate(field, cosine, sine):
    half = field.shape[-1] // 2
    first = field[..., :half]
    second = field[..., half:]
    return jnp.concatenate(
        [first * cosine - second * sine, second * cosine + first * sine], axis=-1
    )


def swiglu(gate, up):
    return jax.nn.silu(gate) * up


def block_mask(segment_row, start, block):
    length = segment_row.shape[0]
    own = lax.dynamic_slice_in_dim(segment_row, start, block, 0)
    places = jnp.arange(length, dtype=jnp.int32)
    own_places = start + jnp.arange(block, dtype=jnp.int32)
    same = own[:, None] == segment_row[None, :]
    live = (own[:, None] < MAXDOCS) | (own_places[:, None] == places[None, :])
    return same & live


def block_scores(query_block, keys, allowed, scale):
    scores = (
        jnp.einsum("qhd,khd->hqk", query_block, keys, preferred_element_type=jnp.float32) * scale
    )
    return jnp.where(allowed[None], scores, NEGATIVE)


def attend_row(queries, keys, values, segment_row):
    length, heads, depth = queries.shape
    block = min(512, length)
    scale = depth ** (-0.5)

    def one_block(start):
        query_block = lax.dynamic_slice_in_dim(queries, start, block, 0)
        scores = block_scores(query_block, keys, block_mask(segment_row, start, block), scale)
        highest = jnp.max(scores, axis=-1, keepdims=True)
        expo = jnp.exp(scores - highest)
        total = jnp.sum(expo, axis=-1, keepdims=True)
        probs = (expo / total).astype(jnp.bfloat16)
        mixed = jnp.einsum("hqk,khd->qhd", probs, values, preferred_element_type=jnp.float32)
        return (mixed.astype(jnp.bfloat16), (highest + jnp.log(total))[..., 0])

    starts = jnp.arange(length // block, dtype=jnp.int32) * block
    mixed, logsum = lax.map(one_block, starts)
    return (mixed.reshape(length, heads, depth), logsum)


def attend_back(queries, keys, values, segment_row, logsum, heads_grad):
    length, heads, depth = queries.shape
    block = min(512, length)
    scale = depth ** (-0.5)

    def one_block(carry, inputs):
        start, block_logsum = inputs
        query_block = lax.dynamic_slice_in_dim(queries, start, block, 0)
        grad_block = lax.dynamic_slice_in_dim(heads_grad, start, block, 0)
        scores = block_scores(query_block, keys, block_mask(segment_row, start, block), scale)
        probs = jnp.exp(scores - block_logsum[..., None])
        probs_grad = jnp.einsum(
            "qhd,khd->hqk", grad_block, values, preferred_element_type=jnp.float32
        )
        weighted = jnp.sum(probs * probs_grad, axis=-1, keepdims=True)
        score_low = (probs * (probs_grad - weighted)).astype(jnp.bfloat16)
        query_grad = (
            jnp.einsum("hqk,khd->qhd", score_low, keys, preferred_element_type=jnp.float32) * scale
        )
        key_grad = (
            carry[0]
            + jnp.einsum("hqk,qhd->khd", score_low, query_block, preferred_element_type=jnp.float32)
            * scale
        )
        value_grad = carry[1] + jnp.einsum(
            "hqk,qhd->khd",
            probs.astype(jnp.bfloat16),
            grad_block,
            preferred_element_type=jnp.float32,
        )
        return ((key_grad, value_grad), query_grad)

    starts = jnp.arange(length // block, dtype=jnp.int32) * block
    zeros = jnp.zeros((length, heads, depth), jnp.float32)
    (key_grad, value_grad), query_grad = lax.scan(one_block, (zeros, zeros), (starts, logsum))
    return (query_grad.reshape(length, heads, depth), key_grad, value_grad)


def per_device(
    layer_input,
    segments,
    qkv_weight,
    out_weight,
    gate_weight,
    up_weight,
    down_weight,
    norm_params,
    cotangent,
):
    piece_len, batch_rows, width = layer_input.shape
    seq_len = piece_len * lax.axis_size("tensor")
    head_dim = HEAD_DIM
    local_heads = out_weight.shape[0] // head_dim
    head_cols = local_heads * head_dim
    positions = jax.vmap(positions_of)(segments)
    cosine, sine = rotary_tables(positions, head_dim)
    cosine = cosine[:, :, None, :]
    sine = sine[:, :, None, :]

    def project_heads(gathered):
        joint = jnp.einsum("srd,dc->rsc", gathered, qkv_weight, preferred_element_type=jnp.float32)
        joint = joint.reshape(batch_rows, seq_len, local_heads, 3, head_dim)
        queries = rotate(joint[:, :, :, 0], cosine, sine).astype(jnp.bfloat16)
        keys = rotate(joint[:, :, :, 1], cosine, sine).astype(jnp.bfloat16)
        return (queries, keys, joint[:, :, :, 2].astype(jnp.bfloat16))

    def feed_forward(gathered):
        gate = jnp.einsum("srd,df->srf", gathered, gate_weight, preferred_element_type=jnp.float32)
        up = jnp.einsum("srd,df->srf", gathered, up_weight, preferred_element_type=jnp.float32)
        return (gate, up)

    gathered_input = lax.all_gather(layer_input, "tensor", axis=0, tiled=True)
    queries, keys, values = project_heads(gathered_input)
    heads_out, logsum = lax.map(lambda parts: attend_row(*parts), (queries, keys, values, segments))
    heads_flat = heads_out.reshape(batch_rows, seq_len, head_cols)
    used = heads_flat
    attention = lax.psum_scatter(
        jnp.einsum("rsc,cd->srd", used, out_weight, preferred_element_type=jnp.float32).astype(
            jnp.bfloat16
        ),
        "tensor",
        scatter_dimension=0,
        tiled=True,
    ).astype(jnp.float32)
    normed, first_pull = jax.vjp(
        layer_norm, layer_input.astype(jnp.float32) + attention, norm_params[0], norm_params[1]
    )
    gathered_norm = lax.all_gather(normed.astype(jnp.bfloat16), "tensor", axis=0, tiled=True)
    gate, up = feed_forward(gathered_norm)
    hidden = swiglu(gate, up).astype(jnp.bfloat16)
    used = hidden
    branch = lax.psum_scatter(
        jnp.einsum("srf,fd->srd", used, down_weight, preferred_element_type=jnp.float32).astype(
            jnp.bfloat16
        ),
        "tensor",
        scatter_dimension=0,
        tiled=True,
    ).astype(jnp.float32)
    output, second_pull = jax.vjp(layer_norm, normed + branch, norm_params[2], norm_params[3])
    second_grad, gain_two, bias_two = second_pull(cotangent.astype(jnp.float32))
    gate_again, up_again = feed_forward(gathered_norm)
    piece = lax.all_gather(second_grad.astype(jnp.bfloat16), "tensor", axis=0, tiled=True)
    rows_grad = jnp.einsum("srd,fd->srf", piece, down_weight, preferred_element_type=jnp.float32)
    hidden_grad = rows_grad
    used = hidden
    down_part = jnp.einsum("srf,srd->fd", used, piece, preferred_element_type=jnp.float32)
    hidden_grad, down_part = (hidden_grad, down_part)
    unused, swiglu_pull = jax.vjp(swiglu, gate_again, up_again)
    gate_full, up_full = swiglu_pull(hidden_grad)
    gate_low = gate_full.astype(jnp.bfloat16)
    up_low = up_full.astype(jnp.bfloat16)
    gate_part = jnp.einsum(
        "srd,srf->df", gathered_norm, gate_low, preferred_element_type=jnp.float32
    )
    up_part = jnp.einsum("srd,srf->df", gathered_norm, up_low, preferred_element_type=jnp.float32)
    term = jnp.einsum("srf,df->srd", gate_low, gate_weight, preferred_element_type=jnp.float32)
    normed_grad = second_grad + lax.psum_scatter(
        (
            term + jnp.einsum("srf,df->srd", up_low, up_weight, preferred_element_type=jnp.float32)
        ).astype(jnp.bfloat16),
        "tensor",
        scatter_dimension=0,
        tiled=True,
    ).astype(jnp.float32)
    first_grad, gain_one, bias_one = first_pull(normed_grad)
    query_again, key_again, value_again = project_heads(gathered_input)
    piece = lax.all_gather(first_grad.astype(jnp.bfloat16), "tensor", axis=0, tiled=True)
    rows_grad = jnp.einsum("srd,cd->rsc", piece, out_weight, preferred_element_type=jnp.float32)
    heads_grad = rows_grad
    used = heads_flat
    out_part = jnp.einsum("rsc,srd->cd", used, piece, preferred_element_type=jnp.float32)
    heads_grad, out_part = (heads_grad, out_part)
    heads_low = heads_grad.astype(jnp.bfloat16).reshape(batch_rows, seq_len, local_heads, head_dim)
    query_grad, key_grad, value_grad = lax.map(
        lambda parts: attend_back(*parts),
        (query_again, key_again, value_again, segments, logsum, heads_low),
    )
    query_raw = rotate(query_grad, cosine, -sine)
    key_raw = rotate(key_grad, cosine, -sine)
    joint_grad = (
        jnp.stack([query_raw, key_raw, value_grad], axis=3)
        .reshape(batch_rows, seq_len, 3 * head_cols)
        .astype(jnp.bfloat16)
    )
    qkv_part = jnp.einsum(
        "srd,rsc->dc", gathered_input, joint_grad, preferred_element_type=jnp.float32
    )
    used = joint_grad
    input_grad = first_grad + lax.psum_scatter(
        jnp.einsum("rsc,dc->srd", used, qkv_weight, preferred_element_type=jnp.float32).astype(
            jnp.bfloat16
        ),
        "tensor",
        scatter_dimension=0,
        tiled=True,
    ).astype(jnp.float32)
    qkv_grad, out_grad, gate_grad, up_grad, down_grad = lax.psum(
        (qkv_part, out_part, gate_part, up_part, down_part), "dp"
    )
    norm_grads = lax.psum(
        jnp.stack([gain_one, bias_one, gain_two, bias_two], axis=0), ("dp", "tensor")
    )
    return (
        output.astype(jnp.bfloat16),
        input_grad,
        qkv_grad,
        out_grad,
        gate_grad,
        up_grad,
        down_grad,
        norm_grads,
    )


def solution(mesh):
    placed = (
        P("tensor", "dp", None),
        P("dp", None),
        P(None, "tensor"),
        P("tensor", None),
        P(None, "tensor"),
        P(None, "tensor"),
        P("tensor", None),
        P(),
        P("tensor", "dp", None),
    )
    return jax.shard_map(
        per_device,
        mesh=mesh,
        in_specs=placed,
        out_specs=(
            P("tensor", "dp", None),
            P("tensor", "dp", None),
            P(None, "tensor"),
            P("tensor", None),
            P(None, "tensor"),
            P(None, "tensor"),
            P("tensor", None),
            P(),
        ),
        check_vma=False,
    )
```

profile of v0, /device:TPU:0, one launch (start us, length us, event | category | flops | bytes accessed | tf_op | source)
XLA Modules:
  0.0 1039.7 jit_solution(2395580110291607030)
XLA Ops:
  13.4 62.3 %all-gather.5.cloned.1.call-done = bf16[2048,1,768]{2,0,1:T(8,128)(2,1)} async-done(((bf16[512,1,768]{2,0,1:T(8,128)(2,1)}), bf16[2048,1,768]{2,0,1:T(8,128)(2,1)}) %all-gather.5.cloned.1.call-update) | async-done | bytes 3145744 | tf_op jit(solution)/shard_map/all_gather | solution.py:158
  82.3 105.2 %while.47 = (s32[]{:T(128)}, bf16[4,512,3,64]{1,3,2,0:T(8,128)(2,1)}, f32[4,3,512]{2,1,0:T(4,128)}, s32[4]{0:T(128)S(1)}, s32[2048]{0:T(1024)S(1)}, /*index=5*/b...) while((s32[]{:T(128)}, ...), condition=%wide.region_6.7_spmd, body=%wide.region_3.6_spmd.sunk | while | flops 847347200 | bytes 43979956 | solution.py:83
  87.0 6.9 fusion.148
  100.6 7.3 fusion.150
  113.3 6.9 fusion.148
  126.9 7.3 fusion.150
  139.5 6.9 fusion.148
  153.2 7.3 fusion.150
  179.5 7.3 fusion.150
  194.5 57.7 %reduce-scatter.5.cloned.1.call-done = bf16[512,1,768]{2,0,1:T(8,128)(2,1)} async-done(((bf16[2048,1,768]{2,0,1:T(8,128)(2,1)}), bf16[512,1,768]{2,0,1:T(8,128)(2,1)}) %reduce-scatter.5.cloned.1.call-update) | async-done | bytes 786448 | tf_op jit(solution)/shard_map/reduce_scatter | solution.py:163
  258.1 63.2 %all-gather.7.cloned.1.call-done = bf16[2048,1,768]{2,0,1:T(8,128)(2,1)} async-done(((bf16[512,1,768]{2,0,1:T(8,128)(2,1)}), bf16[2048,1,768]{2,0,1:T(8,128)(2,1)}) %all-gather.7.cloned.1.call-update) | async-done | bytes 3145744 | tf_op jit(solution)/shard_map/all_gather | solution.py:174
  337.1 59.2 %reduce-scatter.7.cloned.1.call-done = bf16[512,1,768]{2,0,1:T(8,128)(2,1)} async-done(((bf16[2048,1,768]{2,0,1:T(8,128)(2,1)}), bf16[512,1,768]{2,0,1:T(8,128)(2,1)}) %reduce-scatter.7.cloned.1.call-update) | async-done | bytes 786448 | tf_op jit(solution)/shard_map/reduce_scatter | solution.py:178
  403.8 63.5 %all-gather.9.cloned.1.call-done = bf16[2048,1,768]{2,0,1:T(8,128)(2,1)} async-done(((bf16[512,1,768]{2,0,1:T(8,128)(2,1)}), bf16[2048,1,768]{2,0,1:T(8,128)(2,1)}) %all-gather.9.cloned.1.call-update) | async-done | bytes 3145744 | tf_op jit(solution)/shard_map/all_gather | solution.py:189
  467.3 9.5 multiply_convert_fusion.1
  483.6 59.1 %reduce-scatter.9.cloned.1.call-done = bf16[512,1,768]{2,0,1:T(8,128)(2,1)} async-done(((bf16[2048,1,768]{2,0,1:T(8,128)(2,1)}), bf16[512,1,768]{2,0,1:T(8,128)(2,1)}) %reduce-scatter.9.cloned.1.call-update) | async-done | bytes 786448 | tf_op jit(solution)/shard_map/reduce_scatter | solution.py:204
  549.5 63.4 %all-gather.11.cloned.1.call-done = bf16[2048,1,768]{2,0,1:T(8,128)(2,1)} async-done(((bf16[512,1,768]{2,0,1:T(8,128)(2,1)}), bf16[2048,1,768]{2,0,1:T(8,128)(2,1)}) %all-gather.11.cloned.1.call-update) | async-done | bytes 3145744 | tf_op jit(solution)/shard_map/all_gather | solution.py:214
  616.9 191.6 %while.48 = (s32[]{:T(128)}, f32[2048,3,64]{0,2,1:T(8,128)}, f32[2048,3,64]{0,2,1:T(8,128)}, f32[4,512,3,64]{1,0,3,2:T(4,128)}, s32[4]{0:T(128)S(1)}, /*index=5*...) while((s32[]{:T(128)}, f32[2048,3,64]{0,2,1:T(8,128)}, ...), condition=%wide.region_20.21_spmd.clone, body=%wide.region_18.20_spmd.clone.sunk | while | flops 2066710016 | bytes 151975328 | solution.py:121
  663.1 8.6 dynamic_update_slice.33
  708.7 8.6 dynamic_update_slice.33
  754.3 8.6 dynamic_update_slice.33
  799.7 8.6 dynamic_update_slice.33
  819.7 7.1 fusion.48
  841.3 42.9 %psum.47 = f32[4,768]{1,0:T(4,128)} all-reduce(f32[4,768]{1,0:T(4,128)S(1)} %pad_maximum_fusion.2), channel_id=1, replica_groups=mesh['dp'=8,'tensor'=4] {'dp','tensor'}, use_global_device_ids=true, to_apply=%region_31.32 | all-reduce | flops 3072 | bytes 24576 | tf_op jit(solution)/shard_map/psum | solution.py:247
  888.4 134.1 %all-reduce.3.cloned.1.call-done = (f32[768,576]{0,1:T(8,128)}, f32[192,768]{1,0:T(8,128)}, f32[768,768]{1,0:T(8,128)}, f32[768,768]{1,0:T(8,128)}, f32[768,768]{1,0:T(8,128)}) async-done(((f32[768,576]{0,1:T(8,128)}, f32[192,768]{1,0:T(8,128)}, f32[768,768]{1,0:T(8,128)}, f32[768,768]{1,0:T(8,128)}, f32[768,768]{1,0:T(8,128)}), (f32[768,576]{0,1:T(8,128)}, f32[192,768]{1,0:T(8,128)}, f32[768,768]{1,0:T(8,128)}, ...) | async-done | bytes 9437200 | tf_op jit(solution)/shard_map/psum | solution.py:244
  (322 shorter events, 291.8 us)
Async XLA Ops:
  7.2 325.9 %copy-start = (bf16[768,768]{1,0:T(8,128)(2,1)S(1)}, bf16[768,768]{1,0:T(8,128)(2,1)}, u32[]{:S(2)}) copy-start(bf16[768,768]{1,0:T(8,128)(2,1)} %param.19) | copy-start | bytes 3538948
  7.2 68.6 %all-gather.5.cloned.1.call-start = ((), (), s32[]{:S(2)}) async-start(), calls=%async_computation.4 | async-start | bytes 3932160 | tf_op jit(solution)/shard_map/all_gather | solution.py:158
  7.9 244.3 %reduce-scatter.5.cloned.1.call-start = ((), (), s32[]{:S(2)}) async-start(), calls=%async_computation.5 | async-start | bytes 3932160 | tf_op jit(solution)/shard_map/reduce_scatter | solution.py:163
  13.4 67.3 %copy-start.21 = (f32[2048,32]{0,1:T(8,128)}, f32[2048,32]{0,1:T(8,128)S(1)}, u32[]{:S(2)}) copy-start(f32[2048,32]{0,1:T(8,128)S(1)} %get-tuple-element.312) | copy-start | bytes 786436
  193.0 59.2 %copy-start.9 = (bf16[512,1,768]{2,0,1:T(8,128)(2,1)S(1)}, bf16[512,1,768]{2,0,1:T(8,128)(2,1)}, u32[]{:S(2)}) copy-start(bf16[512,1,768]{2,0,1:T(8,128)(2,1)} %param.13) | copy-start | bytes 2359300
  193.0 128.3 %all-gather.7.cloned.1.call-start = ((), (), s32[]{:S(2)}) async-start(), calls=%async_computation.6 | async-start | bytes 3932160 | tf_op jit(solution)/shard_map/all_gather | solution.py:174
  257.8 138.5 %reduce-scatter.7.cloned.1.call-start = ((), (), s32[]{:S(2)}) async-start(), calls=%async_computation.7 | async-start | bytes 3932160 | tf_op jit(solution)/shard_map/reduce_scatter | solution.py:178
  337.1 130.2 %all-gather.9.cloned.1.call-start = ((), (), s32[]{:S(2)}) async-start(), calls=%async_computation.8 | async-start | bytes 3932160 | tf_op jit(solution)/shard_map/all_gather | solution.py:189
  403.8 139.0 %reduce-scatter.9.cloned.1.call-start = ((), (), s32[]{:S(2)}) async-start(), calls=%async_computation.9 | async-start | bytes 3932160 | tf_op jit(solution)/shard_map/reduce_scatter | solution.py:204
  483.5 59.2 %copy-start.11 = (bf16[512,1,768]{2,0,1:T(8,128)(2,1)S(1)}, bf16[512,1,768]{2,0,1:T(8,128)(2,1)}, u32[]{:S(2)}) copy-start(bf16[512,1,768]{2,0,1:T(8,128)(2,1)} %reduce-scatter.5.cloned.1.call-done) | copy-start | bytes 2359300
  483.5 59.2 %copy-start.29 = (f32[512]{0:T(512)S(1)}, f32[512]{0:T(512)}, u32[]{:S(2)}) copy-start(f32[512]{0:T(512)} %copy-done.28) | copy-start | bytes 6148
  483.5 59.2 %copy-start.33 = (f32[512]{0:T(512)S(1)}, f32[512]{0:T(512)}, u32[]{:S(2)}) copy-start(f32[512]{0:T(512)} %copy-done.32) | copy-start | bytes 6148
  483.6 62.6 %copy-start.37 = (f32[512]{0:T(512)S(1)}, f32[512]{0:T(512)}, u32[]{:S(2)}) copy-start(f32[512]{0:T(512)} %copy-done.36) | copy-start | bytes 6148
  483.6 129.4 %all-gather.11.cloned.1.call-start = ((), (), s32[]{:S(2)}) async-start(), calls=%async_computation.10 | async-start | bytes 3932160 | tf_op jit(solution)/shard_map/all_gather | solution.py:214
  547.2 65.8 %copy-start.51 = (bf16[192,768]{1,0:T(8,128)(2,1)S(1)}, bf16[192,768]{1,0:T(8,128)(2,1)}, u32[]{:S(2)}) copy-start(bf16[192,768]{1,0:T(8,128)(2,1)} %param.16) | copy-start | bytes 884740
  547.2 69.7 %copy-start.34 = (f32[512]{0:T(512)}, f32[512]{0:T(512)S(1)}, u32[]{:S(2)}) copy-start(f32[512]{0:T(512)S(1)} %negate_multiply_fusion) | copy-start | bytes 6148
  549.5 334.8 %reduce-scatter.11.cloned.1.call-start = ((), (), s32[]{:S(2)}) async-start(), calls=%async_computation.11 | async-start | bytes 3932160 | tf_op jit(solution)/shard_map/reduce_scatter | solution.py:236
  549.5 67.4 %copy-start.53 = (s32[4]{0:T(128)S(1)}, s32[4]{0:T(128)}, u32[]{:S(2)}) copy-start(s32[4]{0:T(128)} %copy-done.52) | copy-start | bytes 52
  704.1 13.2 %copy-start.5 = (bf16[2048,3,64]{0,2,1:T(8,128)(2,1)S(1)}, bf16[2048,3,64]{0,2,1:T(8,128)(2,1)}, u32[]{:S(2)}) copy-start(bf16[2048,3,64]{0,2,1:T(8,128)(2,1)} %copy-done.4) | copy-start | bytes 2359300 | tf_op jit(solution)/shard_map/while/body/eval_jaxpr/while
  704.2 13.2 %copy-start.8 = (bf16[2048,3,64]{0,2,1:T(8,128)(2,1)S(1)}, bf16[2048,3,64]{0,2,1:T(8,128)(2,1)}, u32[]{:S(2)}) copy-start(bf16[2048,3,64]{0,2,1:T(8,128)(2,1)} %copy-done.7) | copy-start | bytes 2359300 | tf_op jit(solution)/shard_map/while/body/eval_jaxpr/while
  749.7 13.2 %copy-start.5 = (bf16[2048,3,64]{0,2,1:T(8,128)(2,1)S(1)}, bf16[2048,3,64]{0,2,1:T(8,128)(2,1)}, u32[]{:S(2)}) copy-start(bf16[2048,3,64]{0,2,1:T(8,128)(2,1)} %copy-done.4) | copy-start | bytes 2359300 | tf_op jit(solution)/shard_map/while/body/eval_jaxpr/while
  819.7 202.8 %all-reduce.3.cloned.1.call-start = ((), (), s32[]{:S(2)}) async-start(), calls=%async_computation.12 | async-start | bytes 18874368 | tf_op jit(solution)/shard_map/psum | solution.py:244
  840.6 43.7 %copy-start.15 = (f32[512,1,768]{2,0,1:T(8,128)S(1)}, f32[512,1,768]{2,0,1:T(8,128)}, u32[]{:S(2)}) copy-start(f32[512,1,768]{2,0,1:T(8,128)} %copy-done.14) | copy-start | bytes 4718596
  840.6 43.7 %copy-start.35 = (f32[512]{0:T(512)S(1)}, f32[512]{0:T(512)}, u32[]{:S(2)}) copy-start(f32[512]{0:T(512)} %copy-done.34) | copy-start | bytes 6148
  (63 other events, 292.2 us)
Sparse Core Ops, SparseCore 0:
  9.6 66.1 all-gather.4
  193.1 59.0 reduce-scatter.4
  257.9 63.3 all-gather.6
  337.2 59.0 reduce-scatter.6
  403.9 63.3 all-gather.8
  483.7 59.0 reduce-scatter.8
  549.6 63.3 all-gather.10
  819.8 59.9 reduce-scatter.10
  884.7 137.7 all-reduce.2
where the time goes:
time: 1050 us; the launch traced here: 1040 us
  waiting for transfers between devices  563 us (54%)
  matrix products  220 us (21%)
  other arithmetic  98.6 us (9%)
  local copies, waits for them, and re-layouts  72.4 us (7%)
  blocking collectives  42.9 us (4%)
  loops' own time  26.6 us (3%)
  between operations  14.9 us (1%)
    psum x1, waiting for transfers between devices, per_device(): lax.psum((qkv_part, out_part, gate_part, up_part, down_part), 'dp')  134 us
    all_gather x1, waiting for transfers between devices, per_device(): lax.all_gather(second_grad.astype(jnp.bfloat16), 'tensor', axis=0, tiled=...  63.5 us
    all_gather x1, waiting for transfers between devices, per_device(): lax.all_gather(first_grad.astype(jnp.bfloat16), 'tensor', axis=0, tiled=T...  63.4 us
    all_gather x1, waiting for transfers between devices, per_device(): lax.all_gather(normed.astype(jnp.bfloat16), 'tensor', axis=0, tiled=True)  63.2 us
    all_gather x1, waiting for transfers between devices, per_device(): gathered_input = lax.all_gather(layer_input, 'tensor', axis=0, tiled=True)  62.3 us
    reduce_scatter x1, waiting for transfers between devices, per_device(): lax.psum_scatter(jnp.einsum('srf,fd->srd', used, down_weight, preferred_e...  59.2 us
    reduce_scatter x1, waiting for transfers between devices, per_device(): lax.psum_scatter((term + jnp.einsum('srf,df->srd', up_low, up_weight, pre...  59.1 us
    reduce_scatter x1, waiting for transfers between devices, per_device(): lax.psum_scatter(jnp.einsum('rsc,cd->srd', used, out_weight, preferred_el...  57.7 us
  transfers between devices with their start and end apart: 9, of which 8 were waited for; matrix products, arithmetic and copies ran while one was open for 3% of the time, Pallas kernels for 0%

commit v1 on v0

--- a/solution.py
+++ b/solution.py
@@ -1,3 +1,4 @@
+import functools
 import jax
 import jax.numpy as jnp
 from jax import lax
@@ -8,6 +9,13 @@
 EPSILON = 1e-05
 ROPE_BASE = 1000.0
 NEGATIVE = -1e30
+
+
+def measure_skins(incoming_x, along_axis):
+    return lax.all_gather(incoming_x, along_axis).sum(axis=0)
+
+
+_lead_sources_all = functools.partial(measure_skins, along_axis=("dp", "tensor"))
 
 
 def layer_norm(total, gain, bias):
@@ -244,9 +252,7 @@
     qkv_grad, out_grad, gate_grad, up_grad, down_grad = lax.psum(
         (qkv_part, out_part, gate_part, up_part, down_part), "dp"
     )
-    norm_grads = lax.psum(
-        jnp.stack([gain_one, bias_one, gain_two, bias_two], axis=0), ("dp", "tensor")
-    )
+    norm_grads = _lead_sources_all(jnp.stack([gain_one, bias_one, gain_two, bias_two], axis=0))
     return (
         output.astype(jnp.bfloat16),
         input_grad,

time: 1050 us -> 1060 us (level)
  blocking collectives: 42.9 us -> 73.9 us
  waiting for transfers between devices: 563 us -> 536 us
    all_gather x0 -> x1, blocking collectives: none -> 73.9 us  [measure_skins(): return lax.all_gather(incoming_x, along_axis).sum(axis=0)]
    psum x1 -> x0, blocking collectives: 42.9 us -> none  [per_device(): lax.psum(jnp.stack([gain_one, bias_one, gain_two, bias_two], axis=0), ('d...]
    psum x1, waiting for transfers between devices: 134 us -> 106 us  [per_device(): lax.psum((qkv_part, out_part, gate_part, up_part, down_part), 'dp')]
where the time goes in v1:
time: 1060 us; the launch traced here: 1040 us
  waiting for transfers between devices  536 us (51%)
  matrix products  220 us (21%)
  other arithmetic  99.3 us (9%)
  blocking collectives  73.9 us (7%)
  local copies, waits for them, and re-layouts  72.4 us (7%)
  loops' own time  26.6 us (3%)
  between operations  14.9 us (1%)
    psum x1, waiting for transfers between devices, per_device(): lax.psum((qkv_part, out_part, gate_part, up_part, down_part), 'dp')  106 us
    all_gather x1, blocking collectives, measure_skins(): return lax.all_gather(incoming_x, along_axis).sum(axis=0)  73.9 us
    all_gather x1, waiting for transfers between devices, per_device(): lax.all_gather(second_grad.astype(jnp.bfloat16), 'tensor', axis=0, tiled=...  63.5 us
    all_gather x1, waiting for transfers between devices, per_device(): lax.all_gather(first_grad.astype(jnp.bfloat16), 'tensor', axis=0, tiled=T...  63.4 us
    all_gather x1, waiting for transfers between devices, per_device(): lax.all_gather(normed.astype(jnp.bfloat16), 'tensor', axis=0, tiled=True)  63.2 us
    all_gather x1, waiting for transfers between devices, per_device(): gathered_input = lax.all_gather(layer_input, 'tensor', axis=0, tiled=True)  62.3 us
    reduce_scatter x1, waiting for transfers between devices, per_device(): lax.psum_scatter(jnp.einsum('srf,fd->srd', used, down_weight, preferred_e...  59.2 us
    reduce_scatter x1, waiting for transfers between devices, per_device(): lax.psum_scatter((term + jnp.einsum('srf,df->srd', up_low, up_weight, pre...  59.1 us
  transfers between devices with their start and end apart: 9, of which 8 were waited for; matrix products, arithmetic and copies ran while one was open for 3% of the time, Pallas kernels for 0%

profile of v1, /device:TPU:0, one launch (start us, length us, event | category | flops | bytes accessed | tf_op | source)
XLA Modules:
  0.0 1043.6 jit_solution(17039508712609658091)
XLA Ops:
  13.4 62.3 %all-gather.7.cloned.1.call-done = bf16[2048,1,768]{2,0,1:T(8,128)(2,1)} async-done(((bf16[512,1,768]{2,0,1:T(8,128)(2,1)}), bf16[2048,1,768]{2,0,1:T(8,128)(2,1)}) %all-gather.7.cloned.1.call-update) | async-done | bytes 3145744 | tf_op jit(solution)/shard_map/all_gather | solution.py:166
  82.3 105.2 %while.47 = (s32[]{:T(128)}, bf16[4,512,3,64]{1,3,2,0:T(8,128)(2,1)}, f32[4,3,512]{2,1,0:T(4,128)}, s32[4]{0:T(128)S(1)}, s32[2048]{0:T(1024)S(1)}, /*index=5*/b...) while((s32[]{:T(128)}, ...), condition=%wide.region_6.7_spmd, body=%wide.region_3.6_spmd.sunk | while | flops 847347200 | bytes 43979956 | solution.py:91
  87.0 6.9 fusion.148
  100.6 7.3 fusion.150
  113.3 6.9 fusion.148
  126.9 7.3 fusion.150
  139.5 6.9 fusion.148
  153.2 7.3 fusion.150
  179.5 7.3 fusion.150
  194.5 57.7 %reduce-scatter.5.cloned.1.call-done = bf16[512,1,768]{2,0,1:T(8,128)(2,1)} async-done(((bf16[2048,1,768]{2,0,1:T(8,128)(2,1)}), bf16[512,1,768]{2,0,1:T(8,128)(2,1)}) %reduce-scatter.5.cloned.1.call-update) | async-done | bytes 786448 | tf_op jit(solution)/shard_map/reduce_scatter | solution.py:171
  258.1 63.2 %all-gather.9.cloned.1.call-done = bf16[2048,1,768]{2,0,1:T(8,128)(2,1)} async-done(((bf16[512,1,768]{2,0,1:T(8,128)(2,1)}), bf16[2048,1,768]{2,0,1:T(8,128)(2,1)}) %all-gather.9.cloned.1.call-update) | async-done | bytes 3145744 | tf_op jit(solution)/shard_map/all_gather | solution.py:182
  337.1 59.2 %reduce-scatter.7.cloned.1.call-done = bf16[512,1,768]{2,0,1:T(8,128)(2,1)} async-done(((bf16[2048,1,768]{2,0,1:T(8,128)(2,1)}), bf16[512,1,768]{2,0,1:T(8,128)(2,1)}) %reduce-scatter.7.cloned.1.call-update) | async-done | bytes 786448 | tf_op jit(solution)/shard_map/reduce_scatter | solution.py:186
  403.8 63.5 %all-gather.11.cloned.1.call-done = bf16[2048,1,768]{2,0,1:T(8,128)(2,1)} async-done(((bf16[512,1,768]{2,0,1:T(8,128)(2,1)}), bf16[2048,1,768]{2,0,1:T(8,128)(2,1)}) %all-gather.11.cloned.1.call-update) | async-done | bytes 3145744 | tf_op jit(solution)/shard_map/all_gather | solution.py:197
  467.3 9.5 multiply_convert_fusion.1
  483.6 59.1 %reduce-scatter.9.cloned.1.call-done = bf16[512,1,768]{2,0,1:T(8,128)(2,1)} async-done(((bf16[2048,1,768]{2,0,1:T(8,128)(2,1)}), bf16[512,1,768]{2,0,1:T(8,128)(2,1)}) %reduce-scatter.9.cloned.1.call-update) | async-done | bytes 786448 | tf_op jit(solution)/shard_map/reduce_scatter | solution.py:212
  549.5 63.4 %all-gather.13.cloned.1.call-done = bf16[2048,1,768]{2,0,1:T(8,128)(2,1)} async-done(((bf16[512,1,768]{2,0,1:T(8,128)(2,1)}), bf16[2048,1,768]{2,0,1:T(8,128)(2,1)}) %all-gather.13.cloned.1.call-update) | async-done | bytes 3145744 | tf_op jit(solution)/shard_map/all_gather | solution.py:222
  616.9 191.6 %while.48 = (s32[]{:T(128)}, f32[2048,3,64]{0,2,1:T(8,128)}, f32[2048,3,64]{0,2,1:T(8,128)}, f32[4,512,3,64]{1,0,3,2:T(4,128)}, s32[4]{0:T(128)S(1)}, /*index=5*...) while((s32[]{:T(128)}, f32[2048,3,64]{0,2,1:T(8,128)}, ...), condition=%wide.region_20.21_spmd.clone, body=%wide.region_18.20_spmd.clone.sunk | while | flops 2066710016 | bytes 151975328 | solution.py:129
  663.1 8.6 dynamic_update_slice.33
  708.7 8.6 dynamic_update_slice.33
  754.3 8.6 dynamic_update_slice.33
  799.7 8.6 dynamic_update_slice.33
  819.7 7.1 fusion.48
  841.3 73.9 %all-gather.1 = f32[32,4,768]{2,1,0:T(4,128)S(1)} all-gather(f32[1,4,768]{2,1,0:T(4,128)S(1)} %maximum_bitcast_fusion.2), channel_id=2, replica_groups=mesh['dp'=8,'tensor'=4] {'dp','tensor'}, dimensions={0}, use_global_device_ids=true | all-gather | bytes 405504 | tf_op jit(solution)/shard_map/all_gather | solution.py:15
  920.0 106.4 %all-reduce.3.cloned.1.call-done = (f32[768,576]{0,1:T(8,128)}, f32[192,768]{1,0:T(8,128)}, f32[768,768]{1,0:T(8,128)}, f32[768,768]{1,0:T(8,128)}, f32[768,768]{1,0:T(8,128)}) async-done(((f32[768,576]{0,1:T(8,128)}, f32[192,768]{1,0:T(8,128)}, f32[768,768]{1,0:T(8,128)}, f32[768,768]{1,0:T(8,128)}, f32[768,768]{1,0:T(8,128)}), (f32[768,576]{0,1:T(8,128)}, f32[192,768]{1,0:T(8,128)}, f32[768,768]{1,0:T(8,128)}, ...) | async-done | bytes 9437200 | tf_op jit(solution)/shard_map/psum | solution.py:252
  (323 shorter events, 292.5 us)
Async XLA Ops:
  7.2 325.9 %copy-start = (bf16[768,768]{1,0:T(8,128)(2,1)S(1)}, bf16[768,768]{1,0:T(8,128)(2,1)}, u32[]{:S(2)}) copy-start(bf16[768,768]{1,0:T(8,128)(2,1)} %param.19) | copy-start | bytes 3538948
  7.2 68.6 %all-gather.7.cloned.1.call-start = ((), (), s32[]{:S(2)}) async-start(), calls=%async_computation.4 | async-start | bytes 3932160 | tf_op jit(solution)/shard_map/all_gather | solution.py:166
  7.9 244.3 %reduce-scatter.5.cloned.1.call-start = ((), (), s32[]{:S(2)}) async-start(), calls=%async_computation.5 | async-start | bytes 3932160 | tf_op jit(solution)/shard_map/reduce_scatter | solution.py:171
  13.4 67.3 %copy-start.21 = (f32[2048,32]{0,1:T(8,128)}, f32[2048,32]{0,1:T(8,128)S(1)}, u32[]{:S(2)}) copy-start(f32[2048,32]{0,1:T(8,128)S(1)} %get-tuple-element.320) | copy-start | bytes 786436
  193.0 59.2 %copy-start.9 = (bf16[512,1,768]{2,0,1:T(8,128)(2,1)S(1)}, bf16[512,1,768]{2,0,1:T(8,128)(2,1)}, u32[]{:S(2)}) copy-start(bf16[512,1,768]{2,0,1:T(8,128)(2,1)} %param.13) | copy-start | bytes 2359300
  193.0 128.3 %all-gather.9.cloned.1.call-start = ((), (), s32[]{:S(2)}) async-start(), calls=%async_computation.6 | async-start | bytes 3932160 | tf_op jit(solution)/shard_map/all_gather | solution.py:182
  257.8 138.5 %reduce-scatter.7.cloned.1.call-start = ((), (), s32[]{:S(2)}) async-start(), calls=%async_computation.7 | async-start | bytes 3932160 | tf_op jit(solution)/shard_map/reduce_scatter | solution.py:186
  337.1 130.2 %all-gather.11.cloned.1.call-start = ((), (), s32[]{:S(2)}) async-start(), calls=%async_computation.8 | async-start | bytes 3932160 | tf_op jit(solution)/shard_map/all_gather | solution.py:197
  403.8 139.0 %reduce-scatter.9.cloned.1.call-start = ((), (), s32[]{:S(2)}) async-start(), calls=%async_computation.9 | async-start | bytes 3932160 | tf_op jit(solution)/shard_map/reduce_scatter | solution.py:212
  483.5 59.2 %copy-start.11 = (bf16[512,1,768]{2,0,1:T(8,128)(2,1)S(1)}, bf16[512,1,768]{2,0,1:T(8,128)(2,1)}, u32[]{:S(2)}) copy-start(bf16[512,1,768]{2,0,1:T(8,128)(2,1)} %reduce-scatter.5.cloned.1.call-done) | copy-start | bytes 2359300
  483.5 59.2 %copy-start.29 = (f32[512]{0:T(512)S(1)}, f32[512]{0:T(512)}, u32[]{:S(2)}) copy-start(f32[512]{0:T(512)} %copy-done.28) | copy-start | bytes 6148
  483.5 59.2 %copy-start.33 = (f32[512]{0:T(512)S(1)}, f32[512]{0:T(512)}, u32[]{:S(2)}) copy-start(f32[512]{0:T(512)} %copy-done.32) | copy-start | bytes 6148
  483.6 62.6 %copy-start.37 = (f32[512]{0:T(512)S(1)}, f32[512]{0:T(512)}, u32[]{:S(2)}) copy-start(f32[512]{0:T(512)} %copy-done.36) | copy-start | bytes 6148
  483.6 129.4 %all-gather.13.cloned.1.call-start = ((), (), s32[]{:S(2)}) async-start(), calls=%async_computation.10 | async-start | bytes 3932160 | tf_op jit(solution)/shard_map/all_gather | solution.py:222
  547.2 65.8 %copy-start.51 = (bf16[192,768]{1,0:T(8,128)(2,1)S(1)}, bf16[192,768]{1,0:T(8,128)(2,1)}, u32[]{:S(2)}) copy-start(bf16[192,768]{1,0:T(8,128)(2,1)} %param.16) | copy-start | bytes 884740
  547.2 69.7 %copy-start.34 = (f32[512]{0:T(512)}, f32[512]{0:T(512)S(1)}, u32[]{:S(2)}) copy-start(f32[512]{0:T(512)S(1)} %negate_multiply_fusion) | copy-start | bytes 6148
  549.5 366.4 %reduce-scatter.11.cloned.1.call-start = ((), (), s32[]{:S(2)}) async-start(), calls=%async_computation.11 | async-start | bytes 3932160 | tf_op jit(solution)/shard_map/reduce_scatter | solution.py:244
  549.5 67.4 %copy-start.53 = (s32[4]{0:T(128)S(1)}, s32[4]{0:T(128)}, u32[]{:S(2)}) copy-start(s32[4]{0:T(128)} %copy-done.52) | copy-start | bytes 52
  704.1 13.2 %copy-start.5 = (bf16[2048,3,64]{0,2,1:T(8,128)(2,1)S(1)}, bf16[2048,3,64]{0,2,1:T(8,128)(2,1)}, u32[]{:S(2)}) copy-start(bf16[2048,3,64]{0,2,1:T(8,128)(2,1)} %copy-done.4) | copy-start | bytes 2359300 | tf_op jit(solution)/shard_map/while/body/eval_jaxpr/while
  704.2 13.2 %copy-start.8 = (bf16[2048,3,64]{0,2,1:T(8,128)(2,1)S(1)}, bf16[2048,3,64]{0,2,1:T(8,128)(2,1)}, u32[]{:S(2)}) copy-start(bf16[2048,3,64]{0,2,1:T(8,128)(2,1)} %copy-done.7) | copy-start | bytes 2359300 | tf_op jit(solution)/shard_map/while/body/eval_jaxpr/while
  749.7 13.2 %copy-start.5 = (bf16[2048,3,64]{0,2,1:T(8,128)(2,1)S(1)}, bf16[2048,3,64]{0,2,1:T(8,128)(2,1)}, u32[]{:S(2)}) copy-start(bf16[2048,3,64]{0,2,1:T(8,128)(2,1)} %copy-done.4) | copy-start | bytes 2359300 | tf_op jit(solution)/shard_map/while/body/eval_jaxpr/while
  819.7 206.7 %all-reduce.3.cloned.1.call-start = ((), (), s32[]{:S(2)}) async-start(), calls=%async_computation.12 | async-start | bytes 18874368 | tf_op jit(solution)/shard_map/psum | solution.py:252
  840.6 75.3 %copy-start.15 = (f32[512,1,768]{2,0,1:T(8,128)S(1)}, f32[512,1,768]{2,0,1:T(8,128)}, u32[]{:S(2)}) copy-start(f32[512,1,768]{2,0,1:T(8,128)} %copy-done.14) | copy-start | bytes 4718596
  840.6 75.3 %copy-start.35 = (f32[512]{0:T(512)S(1)}, f32[512]{0:T(512)}, u32[]{:S(2)}) copy-start(f32[512]{0:T(512)} %copy-done.34) | copy-start | bytes 6148
  (63 other events, 292.2 us)
Sparse Core Ops, SparseCore 0:
  9.6 66.1 all-gather.6
  193.1 59.0 reduce-scatter.4
  257.9 63.3 all-gather.8
  337.2 59.0 reduce-scatter.6
  403.9 63.3 all-gather.10
  483.7 59.0 reduce-scatter.8
  549.6 63.3 all-gather.12
  819.8 63.1 reduce-scatter.10
  887.8 138.5 all-reduce.2
